TPU v7x, 32 devices: a whole 2x2x4 slice. The times are simulated.
32 devices in a mesh: grp: 2 (over y), ctx: 4 (over x, core), head: 4 (over z).
Axes of the slice: x: 2, y: 2, z: 4, core: 2. Of those that a mesh axis runs over, the one named last changes fastest.
Arguments:
- prompt_hidden: bfloat16 [4, 1024, 4096], P('grp', 'ctx', 'head'), parts along dimension 0, may hold values from -3 to 3
- qkv_weight: bfloat16 [3, 4096, 4096], P(None, 'ctx', 'head'), may hold values from -0.09375 to 0.09375
- out_weight: bfloat16 [4096, 4096], P('head', 'ctx'), may hold values from -0.9375 to 0.9375
- embed_table: bfloat16 [32768, 4096], P('ctx', 'head'), may hold values from -60 to 60
- response_ids: int32 [4, 256], P(None, 'grp'), parts along dimension 1, may hold values from 0 to 32767
- assignment: int32 [256], P('grp'), parts along dimension 0, may hold values from 0 to 1
Outputs:
- final_hidden: bfloat16 [4, 256, 4096], P(None, ('grp', 'ctx'), 'head'), parts along dimension 1
There are 2 independent parts, one for each index of `grp`. A program takes and returns all parts, laid end to end along the dimension named above; an argument that names none is the same for every part. Nothing has to cross between parts.
All inputs are finite; a program needn't handle non-finite values.
Results may differ from a plain program's by a relative error of at most 0.023.
Values may be sent and summed in bfloat16 or wider, within the bound.
A program may use at most 128 MiB of HBM per device.

v0:
```python
import jax
import jax.numpy as jnp
from jax import lax
from jax.sharding import PartitionSpec as P

DH = 128


def rms_rows(values):
    return values * lax.rsqrt(jnp.mean(values * values, axis=-1, keepdims=True) + 1e-06)


def on_device(prompt_hidden, qkv_weight, out_weight, embed_table, response_ids, assignment):
    local_cols = prompt_hidden.shape[2]
    prompt_rows = prompt_hidden.shape[1]
    head_size = DH
    local_heads = local_cols // head_size
    steps = response_ids.shape[0]
    resp_local = response_ids.shape[1] // lax.axis_size("ctx")
    ctx_index = lax.axis_index("ctx")
    full_rows = lax.all_gather(qkv_weight, "ctx", axis=1, tiled=True)
    kv_weight = jnp.concatenate([full_rows[1], full_rows[2]], axis=1)
    piece = lax.all_gather(prompt_hidden, "head", axis=2, tiled=True)
    flat_piece = piece.reshape(2 * prompt_rows, piece.shape[2])
    kv_local = jnp.dot(flat_piece, kv_weight, preferred_element_type=jnp.float32)
    kv_local = kv_local.astype(jnp.bfloat16).reshape(2, prompt_rows, 2, local_heads, head_size)
    partial_state = jnp.einsum(
        "pthd,pthe->phde", kv_local[:, :, 0], kv_local[:, :, 1], preferred_element_type=jnp.float32
    )
    state = lax.psum(partial_state.astype(jnp.bfloat16), "ctx").astype(jnp.float32)
    vocab_rows = embed_table.shape[0]
    offset_ids = response_ids - ctx_index * vocab_rows
    inside = (offset_ids >= 0) & (offset_ids < vocab_rows)
    looked = jnp.take(embed_table, jnp.clip(offset_ids, 0, vocab_rows - 1), axis=0)
    looked = jnp.where(inside[:, :, None], looked.astype(jnp.float32), 0.0)
    embedded_mine = lax.psum_scatter(
        looked.astype(jnp.bfloat16), "ctx", scatter_dimension=1, tiled=True
    )
    embedded = lax.all_gather(embedded_mine, "head", axis=2, tiled=True)
    normed = rms_rows(embedded.astype(jnp.float32)).astype(jnp.bfloat16)
    projected_qkv = jnp.einsum(
        "trd,kde->trke", normed, full_rows, preferred_element_type=jnp.float32
    ).astype(jnp.bfloat16)
    projected_qkv = projected_qkv.reshape(steps, resp_local, 3, local_heads, head_size)
    query = projected_qkv[:, :, 0]
    key = projected_qkv[:, :, 1]
    value = projected_qkv[:, :, 2]
    my_prompt = lax.dynamic_slice_in_dim(assignment, ctx_index * resp_local, resp_local, 0)
    query_f = query.astype(jnp.float32)
    both = jnp.einsum("trhd,phde->ptrhe", query_f, state, precision=lax.Precision.HIGHEST)
    chosen = jnp.where((my_prompt == 0)[None, :, None, None], both[0], both[1])
    scores = jnp.einsum("trhd,srhd->rhts", query, key, preferred_element_type=jnp.float32)
    later = jnp.arange(steps)[:, None] >= jnp.arange(steps)[None, :]
    scores = jnp.where(later[None, None], scores, 0.0).astype(jnp.bfloat16)
    local = jnp.einsum("rhts,srhd->trhd", scores, value, preferred_element_type=jnp.float32)
    head_out = rms_rows(chosen + local).astype(jnp.bfloat16).reshape(steps, resp_local, local_cols)
    terms = jnp.einsum(
        "trd,de->tre",
        head_out,
        lax.all_gather(out_weight, "ctx", axis=1, tiled=True),
        preferred_element_type=jnp.float32,
    )
    width = terms.shape[2]
    mine = lax.psum_scatter(
        terms.astype(jnp.bfloat16), "head", scatter_dimension=2, tiled=True
    ).astype(jnp.float32)
    mixed = embedded_mine.astype(jnp.float32) + mine
    squares = lax.psum(jnp.sum(mixed * mixed, axis=-1), "head")
    result = mixed * lax.rsqrt(squares[:, :, None] / width + 1e-06)
    return result.astype(jnp.bfloat16)


def solution(mesh):
    return jax.shard_map(
        on_device,
        mesh=mesh,
        in_specs=(
            P("grp", "ctx", "head"),
            P(None, "ctx", "head"),
            P("head", "ctx"),
            P("ctx", "head"),
            P(None, "grp"),
            P("grp"),
        ),
        out_specs=P(None, ("grp", "ctx"), "head"),
        check_vma=False,
    )
```

profile of v0, /device:TPU:0, one launch (start us, length us, event | category | flops | bytes accessed | tf_op | source)
XLA Modules:
  0.0 461.3 jit_solution(4606842393122182999)
XLA Ops:
  6.5 0.0 reduce-scatter.3.cloned.1.call-start
  6.5 0.7 compare_and_fusion.1
  7.2 0.7 fusion.41
  7.9 10.7 %gather_fusion = bf16[512,1024]{1,0:T(8,128)(2,1)S(1)} fusion(bf16[8192,1024]{1,0:T(8,128)(2,1)} %param.9, s32[1024]{0:T(1024)S(1)} %pad_clamp_fusion), kind=kCustom, calls=%fused_computation | custom fusion | bytes 2099200 | tf_op jit(solution)/shard_map/jit(_take)/gather | solution.py:34
  18.6 1.4 select_convert_fusion
  20.0 0.0 reduce-scatter.3.cloned.1.call-update
  20.0 0.0 all-gather.5.cloned.1.call-start
  20.0 0.7 all-gather.5.cloned.1.call-update
  20.7 0.0 all-gather.7.cloned.1.call-start
  20.8 0.7 all-gather.7.cloned.1.call-update
  21.5 0.0 all-gather.9.cloned.1.call-start
  21.5 26.1 %reduce-scatter.3.cloned.1.call-done = bf16[4,32,1024]{2,1,0:T(8,128)(2,1)} async-done(((bf16[4,128,1024]{2,1,0:T(8,128)(2,1)}), bf16[4,32,1024]{2,1,0:T(8,128)(2,1)}) %reduce-scatter.3.cloned.1.call-update) | async-done | bytes 262160 | tf_op jit(solution)/shard_map/reduce_scatter | solution.py:36
  47.7 0.0 all-gather.9.cloned.1.call-update
  47.7 0.2 all-reduce.2.cloned.1.call-start
  47.9 156.1 %all-gather.5.cloned.1.call-done = bf16[3,4096,1024]{2,1,0:T(8,128)(2,1)} async-done(((bf16[3,1024,1024]{2,1,0:T(8,128)(2,1)}), bf16[3,4096,1024]{2,1,0:T(8,128)(2,1)}) %all-gather.5.cloned.1.call-update) | async-done | bytes 25165840 | tf_op jit(solution)/shard_map/all_gather | solution.py:21
  204.0 11.8 %slice_bitcast_fusion.1 = (bf16[4096,1024]{1,0:T(8,128)(2,1)}, bf16[4096,1024]{1,0:T(8,128)(2,1)}) fusion(bf16[3,4096,1024]{2,1,0:T(8,128)(2,1)} %all-gather.5.cloned.1.call-done), kind=kLoop, calls=%fused_computation.8 | loop fusion | bytes 33554432 | tf_op jit(solution)/shard_map/squeeze | solution.py:22
  215.9 70.5 %all-gather.7.cloned.1.call-done = bf16[2,256,4096]{2,1,0:T(8,128)(2,1)} async-done(((bf16[2,256,1024]{2,1,0:T(8,128)(2,1)}), bf16[2,256,4096]{2,1,0:T(8,128)(2,1)}) %all-gather.7.cloned.1.call-update) | async-done | bytes 4194320 | tf_op jit(solution)/shard_map/all_gather | solution.py:23
  286.4 17.3 %fusion.14 = bf16[512,2048]{0,1:T(8,128)(2,1)} fusion(bf16[512,4096]{1,0:T(8,128)(2,1)} %bitcast.86, bf16[4096,1024]{1,0:T(8,128)(2,1)} %get-tuple-element.8, bf16[4096,1024]{1,0:T(8,128)(2,1)} %get-tuple-element.7), kind=kOutput, calls=%fused_computation.13 | convolution fusion | flops 8624537600 | bytes 23068672 | tf_op jit(solution)/shard_map/dot_general | solution.py:25
  303.7 0.0 copy-start.1
  303.7 2.6 reshape.52
  306.3 1.5 slice_bitcast_fusion.3
  307.8 1.3 convolution_convert_fusion
  309.1 0.0 all-reduce.2.cloned.1.call-update
  309.1 0.0 all-gather.11.cloned.1.call-start
  309.1 0.5 all-gather.11.cloned.1.call-update
  309.7 0.3 reduce-scatter.5.cloned.1.call-start
  310.0 0.0 copy-done.1
  310.0 0.1 dynamic-slice_compare_fusion
  310.0 4.3 all-gather.9.cloned.1.call-done
  314.3 1.5 fusion.17
  315.9 12.1 %fusion.19 = bf16[4,32,3,1024]{3,1,2,0:T(8,128)(2,1)S(1)} fusion(bf16[3,4096,1024]{2,1,0:T(8,128)(2,1)} %all-gather.5.cloned.1.call-done, bf16[4,32,4096]{2,1,0:T(8,128)(2,1)} %all-gather.9.cloned.1.call-done, f32[4,32]{1,0:T(4,128)S(1)} %add_rsqrt_fusion.2), kind=kOutput, calls=%fused_computation.19 | convolution fusion | flops 3223191552 | bytes 27001344 | tf_op jit(solution)/shard_map/trd,kde->trke/dot_general | solution.py:41
  327.9 0.2 copy.28
  328.1 0.2 fusion.45
  328.3 0.7 fusion.23
  329.0 0.0 copy-start
  329.0 20.3 %all-reduce.2.cloned.1.call-done = bf16[2,8,128,128]{3,2,0,1:T(8,128)(2,1)} async-done(((bf16[2,8,128,128]{3,2,0,1:T(8,128)(2,1)}), bf16[2,8,128,128]{3,2,0,1:T(8,128)(2,1)}) %all-reduce.2.cloned.1.call-update) | async-done | bytes 524304 | tf_op jit(solution)/shard_map/psum | solution.py:30
  349.3 1.3 convolution_bitcast_fusion
  350.7 0.4 multiply_reduce_fusion.1
  351.1 58.0 %all-gather.11.cloned.1.call-done = bf16[1024,4096]{1,0:T(8,128)(2,1)} async-done(((bf16[1024,1024]{1,0:T(8,128)(2,1)}), bf16[1024,4096]{1,0:T(8,128)(2,1)}) %all-gather.11.cloned.1.call-update) | async-done | bytes 8388624 | tf_op jit(solution)/shard_map/all_gather | solution.py:60
  409.2 5.7 %fusion.8 = bf16[4,32,4096]{2,1,0:T(8,128)(2,1)} fusion(bf16[1024,4096]{1,0:T(8,128)(2,1)} %all-gather.11.cloned.1.call-done, f32[4,32,8,128]{3,1,0,2:T(8,128)S(1)} %get-tuple-element.6, f32[4,32,8]{1,0,2:T(4,128)S(1)} %add_rsqrt_fusion), kind=kOutput, calls=%fused_computation.11 | convolution fusion | flops 1074528256 | bytes 9965568 | tf_op jit(solution)/shard_map/trd,de->tre/dot_general | solution.py:57
  414.8 0.0 reduce-scatter.5.cloned.1.call-update
  414.9 27.4 %reduce-scatter.5.cloned.1.call-done = bf16[4,32,1024]{2,1,0:T(8,128)(2,1)} async-done(((bf16[4,32,4096]{2,1,0:T(8,128)(2,1)}), bf16[4,32,1024]{2,1,0:T(8,128)(2,1)}) %reduce-scatter.5.cloned.1.call-update) | async-done | bytes 262160 | tf_op jit(solution)/shard_map/reduce_scatter | solution.py:64
  442.3 0.0 copy-done
  442.3 1.1 multiply_reduce_fusion
  443.4 9.3 %psum.15 = f32[4,32]{1,0:T(4,128)S(1)} all-reduce(f32[4,32]{1,0:T(4,128)S(1)} %multiply_reduce_fusion), channel_id=1, replica_groups=mesh['grp'=2,'ctx'=4,'head'=4] {'head'}, use_global_device_ids=true, to_apply=%region_6.7 | all-reduce | flops 128 | bytes 1024 | tf_op jit(solution)/shard_map/psum | solution.py:68
  452.7 1.8 multiply_convert_fusion
  (5 shorter events, 0.0 us)
Async XLA Ops:
  6.5 41.1 %reduce-scatter.3.cloned.1.call-start = ((), (), s32[]{:S(2)}) async-start(), calls=%async_computation.2 | async-start | bytes 1310720 | tf_op jit(solution)/shard_map/reduce_scatter | solution.py:36
  20.0 184.1 %all-gather.5.cloned.1.call-start = ((), (), s32[]{:S(2)}) async-start(), calls=%async_computation.3 | async-start | bytes 31457280 | tf_op jit(solution)/shard_map/all_gather | solution.py:21
  20.7 265.7 %all-gather.7.cloned.1.call-start = ((), (), s32[]{:S(2)}) async-start(), calls=%async_computation.4 | async-start | bytes 5242880 | tf_op jit(solution)/shard_map/all_gather | solution.py:23
  21.5 292.8 %all-gather.9.cloned.1.call-start = ((), (), s32[]{:S(2)}) async-start(), calls=%async_computation.6 | async-start | bytes 1310720 | tf_op jit(solution)/shard_map/all_gather | solution.py:39
  47.7 301.7 %all-reduce.2.cloned.1.call-start = ((), (), s32[]{:S(2)}) async-start(), calls=%async_computation.5 | async-start | bytes 1048576 | tf_op jit(solution)/shard_map/psum | solution.py:30
  303.7 6.2 %copy-start.1 = (s32[128]{0:T(128)S(1)}, s32[128]{0:T(128)}, u32[]{:S(2)}) copy-start(s32[128]{0:T(128)} %param.11) | copy-start | bytes 1540
  309.1 100.1 %all-gather.11.cloned.1.call-start = ((), (), s32[]{:S(2)}) async-start(), calls=%async_computation.7 | async-start | bytes 10485760 | tf_op jit(solution)/shard_map/all_gather | solution.py:60
  309.7 132.6 %reduce-scatter.5.cloned.1.call-start = ((), (), s32[]{:S(2)}) async-start(), calls=%async_computation.8 | async-start | bytes 1310720 | tf_op jit(solution)/shard_map/reduce_scatter | solution.py:64
  329.0 113.3 %copy-start = (bf16[4,32,1024]{2,1,0:T(8,128)(2,1)S(1)}, bf16[4,32,1024]{2,1,0:T(8,128)(2,1)}, u32[]{:S(2)}) copy-start(bf16[4,32,1024]{2,1,0:T(8,128)(2,1)} %reduce-scatter.3.cloned.1.call-done) | copy-start | bytes 786436
Sparse Core Ops, SparseCore 0:
  20.1 27.4 reduce-scatter.2
  49.2 154.7 all-gather.4
  205.6 80.7 all-gather.6
  287.8 26.4 all-gather.8
  316.5 32.7 all-reduce.1
  350.8 58.3 all-gather.10
  415.0 27.2 reduce-scatter.4
where the time goes:
time: 462 us; the launch traced here: 461 us
  waiting for transfers between devices  365 us (79%)
  matrix products  38.4 us (8%)
  local copies, waits for them, and re-layouts  26.9 us (6%)
  between operations  13.6 us (3%)
  blocking collectives  9.28 us (2%)
  other arithmetic  7.7 us (2%)
    all_gather x1, waiting for transfers between devices, on_device(): full_rows = lax.all_gather(qkv_weight, 'ctx', axis=1, tiled=True)  156 us
    all_gather x1, waiting for transfers between devices, on_device(): piece = lax.all_gather(prompt_hidden, 'head', axis=2, tiled=True)  70.5 us
    all_gather x1, waiting for transfers between devices, on_device(): lax.all_gather(out_weight, 'ctx', axis=1, tiled=True)  58 us
    reduce_scatter x1, waiting for transfers between devices, on_device(): lax.psum_scatter(terms.astype(jnp.bfloat16), 'head', scatter_dimension=2,...  27.4 us
    reduce_scatter x1, waiting for transfers between devices, on_device(): lax.psum_scatter(looked.astype(jnp.bfloat16), 'ctx', scatter_dimension=1,...  26.1 us
    psum x1, waiting for transfers between devices, on_device(): lax.psum(partial_state.astype(jnp.bfloat16), 'ctx').astype(jnp.float32)  20.3 us
    dot_general x1, matrix products, on_device(): jnp.dot(flat_piece, kv_weight, preferred_element_type=jnp.float32)  17.3 us
    dot_general x1, matrix products, on_device(): jnp.einsum('trd,kde->trke', normed, full_rows, preferred_element_type=jnp...  12.1 us
  transfers between devices with their start and end apart: 7, of which 7 were waited for; matrix products, arithmetic and copies ran while one was open for 11% of the time, Pallas kernels for 0%

commit v1 on v0

--- a/solution.py
+++ b/solution.py
@@ -20,7 +20,12 @@
     ctx_index = lax.axis_index("ctx")
     full_rows = lax.all_gather(qkv_weight, "ctx", axis=1, tiled=True)
     kv_weight = jnp.concatenate([full_rows[1], full_rows[2]], axis=1)
-    piece = lax.all_gather(prompt_hidden, "head", axis=2, tiled=True)
+    ring = [prompt_hidden]
+    for hop in range(3):
+        ring.append(lax.ppermute(ring[-1], "head", [(dev, (dev + 1) % 4) for dev in range(4)]))
+    piece = jnp.roll(
+        jnp.concatenate(ring[::-1], axis=2), (lax.axis_index("head") + 1) * ring[0].shape[2], axis=2
+    )
     flat_piece = piece.reshape(2 * prompt_rows, piece.shape[2])
     kv_local = jnp.dot(flat_piece, kv_weight, preferred_element_type=jnp.float32)
     kv_local = kv_local.astype(jnp.bfloat16).reshape(2, prompt_rows, 2, local_heads, head_size)

time: 462 us -> 381 us (0.82)
  waiting for transfers between devices: 365 us -> 280 us
    ppermute x0 -> x3, waiting for transfers between devices: none -> 76.4 us  [on_device(): lax.ppermute(ring[-1], 'head', [(dev, (dev + 1) % 4) for dev in range(4)])]
    all_gather x1 -> x0, waiting for transfers between devices: 70.5 us -> none  [on_device(): piece = lax.all_gather(prompt_hidden, 'head', axis=2, tiled=True)]
    all_gather x1, waiting for transfers between devices: 156 us -> 98.2 us  [on_device(): full_rows = lax.all_gather(qkv_weight, 'ctx', axis=1, tiled=True)]
    reduce_scatter x1, waiting for transfers between devices: 26.1 us -> 0.01 us  [on_device(): lax.psum_scatter(looked.astype(jnp.bfloat16), 'ctx', scatter_dimension=1,...]
  transfers between devices with their start and end apart: 7 -> 9, of which waited for: 7 -> 7; matrix products, arithmetic and copies ran while one was open for 11% -> 14% of each run, Pallas kernels for 0% -> 0%
where the time goes in v1:
time: 381 us
  waiting for transfers between devices  280 us (73%)
  matrix products  37.2 us (10%)
  local copies, waits for them, and re-layouts  28.9 us (8%)
  between operations  13.7 us (4%)
  blocking collectives  9.28 us (2%)
  other arithmetic  7.72 us (2%)
    all_gather x1, waiting for transfers between devices, on_device(): full_rows = lax.all_gather(qkv_weight, 'ctx', axis=1, tiled=True)  98.2 us
    ppermute x3, waiting for transfers between devices, on_device(): lax.ppermute(ring[-1], 'head', [(dev, (dev + 1) % 4) for dev in range(4)])  76.4 us
    all_gather x1, waiting for transfers between devices, on_device(): lax.all_gather(out_weight, 'ctx', axis=1, tiled=True)  58 us
    reduce_scatter x1, waiting for transfers between devices, on_device(): lax.psum_scatter(terms.astype(jnp.bfloat16), 'head', scatter_dimension=2,...  27.4 us
    psum x1, waiting for transfers between devices, on_device(): lax.psum(partial_state.astype(jnp.bfloat16), 'ctx').astype(jnp.float32)  18.9 us
    dot_general x1, matrix products, on_device(): jnp.dot(flat_piece, kv_weight, preferred_element_type=jnp.float32)  15.9 us
    dot_general x1, matrix products, on_device(): jnp.einsum('trd,kde->trke', normed, full_rows, preferred_element_type=jnp...  12.1 us
    squeeze x1, local copies, waits for them, and re-layouts, on_device(): kv_weight = jnp.concatenate([full_rows[1], full_rows[2]], axis=1)  11.6 us
  transfers between devices with their start and end apart: 9, of which 7 were waited for; matrix products, arithmetic and copies ran while one was open for 14% of the time, Pallas kernels for 0%

profile of v1, /device:TPU:0, one launch (start us, length us, event | category | flops | bytes accessed | tf_op | source)
XLA Modules:
  0.0 380.7 jit_solution(3156584296003578839)
XLA Ops:
  6.5 0.7 compare_and_fusion.1
  7.2 0.7 fusion.41
  7.9 10.7 %gather_fusion = bf16[512,1024]{1,0:T(8,128)(2,1)S(1)} fusion(bf16[8192,1024]{1,0:T(8,128)(2,1)} %param.9, s32[1024]{0:T(1024)S(1)} %pad_clamp_fusion), kind=kCustom, calls=%fused_computation | custom fusion | bytes 2099200 | tf_op jit(solution)/shard_map/jit(_take)/gather | solution.py:39
  18.7 1.4 select_convert_fusion
  20.1 0.0 reduce-scatter.3.cloned.1.call-update
  20.1 0.0 all-gather.4.cloned.1.call-start
  20.2 0.7 all-gather.4.cloned.1.call-update
  20.9 0.0 all-gather.6.cloned.1.call-start
  20.9 3.1 collective-permute-start
  24.0 25.2 %collective-permute-done = bf16[2,256,1024]{2,1,0:T(8,128)(2,1)S(1)} collective-permute-done((bf16[2,256,1024]{2,1,0:T(8,128)(2,1)S(1)}, bf16[2,256,1024]{2,1,0:T(8,128)(2,1)S(1)}, u32[]{:S(2)}, u32[]{:S(2)}) %collective-permute-start) | collective-permute-done | bytes 1048608 | tf_op jit(solution)/shard_map/ppermute | solution.py:25
  49.2 26.1 %collective-permute-done.1 = bf16[2,256,1024]{2,1,0:T(8,128)(2,1)S(1)} collective-permute-done((bf16[2,256,1024]{2,1,0:T(8,128)(2,1)S(1)}, bf16[2,256,1024]{2,1,0:T(8,128)(2,1)S(1)}, u32[]{:S(2)}, u32[]{:S(2)}) %collective-permute-start.1) | collective-permute-done | bytes 1048608 | tf_op jit(solution)/shard_map/ppermute | solution.py:25
  75.3 0.0 all-gather.6.cloned.1.call-update
  75.4 0.2 all-reduce.2.cloned.1.call-start
  75.6 25.1 %collective-permute-done.2 = bf16[2,256,1024]{2,1,0:T(8,128)(2,1)} collective-permute-done((bf16[2,256,1024]{2,1,0:T(8,128)(2,1)S(1)}, bf16[2,256,1024]{2,1,0:T(8,128)(2,1)}, u32[]{:S(2)}, u32[]{:S(2)}) %collective-permute-start.2) | collective-permute-done | bytes 1048608 | tf_op jit(solution)/shard_map/ppermute | solution.py:25
  100.7 1.3 constant_dynamic-update-slice_fusion.7
  102.0 0.1 constant_dynamic-update-slice_fusion.6
  102.1 0.1 constant_dynamic-update-slice_fusion.5
  102.1 0.1 constant_dynamic-update-slice_fusion.4
  102.2 1.3 constant_dynamic-update-slice_fusion.3
  103.6 0.1 constant_dynamic-update-slice_fusion.2
  103.6 0.1 constant_dynamic-update-slice_fusion.1
  103.7 0.1 constant_dynamic-update-slice_fusion
  103.8 2.2 constant_dynamic-slice_fusion
  106.0 98.2 %all-gather.4.cloned.1.call-done = bf16[3,4096,1024]{2,1,0:T(8,128)(2,1)} async-done(((bf16[3,1024,1024]{2,1,0:T(8,128)(2,1)}), bf16[3,4096,1024]{2,1,0:T(8,128)(2,1)}) %all-gather.4.cloned.1.call-update) | async-done | bytes 25165840 | tf_op jit(solution)/shard_map/all_gather | solution.py:21
  204.2 11.6 %slice_bitcast_fusion.1 = (bf16[4096,1024]{1,0:T(8,128)(2,1)}, bf16[4096,1024]{1,0:T(8,128)(2,1)}) fusion(bf16[3,4096,1024]{2,1,0:T(8,128)(2,1)} %all-gather.4.cloned.1.call-done), kind=kLoop, calls=%fused_computation.8 | loop fusion | bytes 33554432 | tf_op jit(solution)/shard_map/squeeze | solution.py:22
  215.8 15.9 %fusion.16 = bf16[64,8,16,128]{3,1,2,0:T(8,128)(2,1)S(1)} fusion(bf16[512,4096]{1,0:T(8,128)(2,1)} %bitcast.86, bf16[4096,1024]{1,0:T(8,128)(2,1)} %get-tuple-element.8, bf16[4096,1024]{1,0:T(8,128)(2,1)} %get-tuple-element.7), kind=kOutput, calls=%fused_computation.18 | convolution fusion | flops 8624537600 | bytes 23068672 | tf_op jit(solution)/shard_map/dot_general | solution.py:30
  231.7 0.6 copy.28
  232.3 0.4 slice_bitcast_fusion.3
  232.7 1.5 convolution_convert_fusion
  234.2 0.0 all-reduce.2.cloned.1.call-update
  234.2 0.0 all-gather.8.cloned.1.call-start
  234.2 0.5 all-gather.8.cloned.1.call-update
  234.8 0.3 reduce-scatter.5.cloned.1.call-start
  235.1 0.1 dynamic-slice_compare_fusion
  235.2 1.5 fusion.14
  236.7 12.1 %fusion.19 = bf16[4,32,3,1024]{3,1,2,0:T(8,128)(2,1)S(1)} fusion(bf16[3,4096,1024]{2,1,0:T(8,128)(2,1)} %all-gather.4.cloned.1.call-done, bf16[4,32,4096]{2,1,0:T(8,128)(2,1)} %all-gather.6.cloned.1.call-done, f32[4,32]{1,0:T(4,128)S(1)} %add_rsqrt_fusion.2), kind=kOutput, calls=%fused_computation.19 | convolution fusion | flops 3223191552 | bytes 27001344 | tf_op jit(solution)/shard_map/trd,kde->trke/dot_general | solution.py:46
  248.8 0.2 copy.29
  249.0 0.2 fusion.45
  249.1 0.7 fusion.23
  249.9 18.9 %all-reduce.2.cloned.1.call-done = bf16[2,8,128,128]{3,2,0,1:T(8,128)(2,1)} async-done(((bf16[2,8,128,128]{3,2,0,1:T(8,128)(2,1)}), bf16[2,8,128,128]{3,2,0,1:T(8,128)(2,1)}) %all-reduce.2.cloned.1.call-update) | async-done | bytes 524304 | tf_op jit(solution)/shard_map/psum | solution.py:35
  268.8 1.3 convolution_bitcast_fusion
  270.1 0.4 multiply_reduce_fusion.1
  270.6 58.0 %all-gather.8.cloned.1.call-done = bf16[1024,4096]{1,0:T(8,128)(2,1)} async-done(((bf16[1024,1024]{1,0:T(8,128)(2,1)}), bf16[1024,4096]{1,0:T(8,128)(2,1)}) %all-gather.8.cloned.1.call-update) | async-done | bytes 8388624 | tf_op jit(solution)/shard_map/all_gather | solution.py:65
  328.6 5.7 %fusion.8 = bf16[4,32,4096]{2,1,0:T(8,128)(2,1)} fusion(bf16[1024,4096]{1,0:T(8,128)(2,1)} %all-gather.8.cloned.1.call-done, f32[4,32,8,128]{3,1,0,2:T(8,128)S(1)} %get-tuple-element.6, f32[4,32,8]{1,0,2:T(4,128)S(1)} %add_rsqrt_fusion), kind=kOutput, calls=%fused_computation.11 | convolution fusion | flops 1074528256 | bytes 9965568 | tf_op jit(solution)/shard_map/trd,de->tre/dot_general | solution.py:62
  334.3 27.4 %reduce-scatter.5.cloned.1.call-done = bf16[4,32,1024]{2,1,0:T(8,128)(2,1)} async-done(((bf16[4,32,4096]{2,1,0:T(8,128)(2,1)}), bf16[4,32,1024]{2,1,0:T(8,128)(2,1)}) %reduce-scatter.5.cloned.1.call-update) | async-done | bytes 262160 | tf_op jit(solution)/shard_map/reduce_scatter | solution.py:69
  361.7 1.1 multiply_reduce_fusion
  362.8 9.3 %psum.15 = f32[4,32]{1,0:T(4,128)S(1)} all-reduce(f32[4,32]{1,0:T(4,128)S(1)} %multiply_reduce_fusion), channel_id=1, replica_groups=mesh['grp'=2,'ctx'=4,'head'=4] {'head'}, use_global_device_ids=true, to_apply=%region_6.7 | all-reduce | flops 128 | bytes 1024 | tf_op jit(solution)/shard_map/psum | solution.py:73
  372.1 1.8 multiply_convert_fusion
  (17 shorter events, 0.1 us)
Async XLA Ops:
  6.5 68.8 %reduce-scatter.3.cloned.1.call-start = ((), (), s32[]{:S(2)}) async-start(), calls=%async_computation.2 | async-start | bytes 1310720 | tf_op jit(solution)/shard_map/reduce_scatter | solution.py:41
  7.9 13.0 %copy-start = (bf16[2,256,1024]{2,1,0:T(8,128)(2,1)S(1)}, bf16[2,256,1024]{2,1,0:T(8,128)(2,1)}, u32[]{:S(2)}) copy-start(bf16[2,256,1024]{2,1,0:T(8,128)(2,1)} %param.6) | copy-start | bytes 3145732
  20.1 184.1 %all-gather.4.cloned.1.call-start = ((), (), s32[]{:S(2)}) async-start(), calls=%async_computation.3 | async-start | bytes 31457280 | tf_op jit(solution)/shard_map/all_gather | solution.py:21
  20.9 214.3 %all-gather.6.cloned.1.call-start = ((), (), s32[]{:S(2)}) async-start(), calls=%async_computation.5 | async-start | bytes 1310720 | tf_op jit(solution)/shard_map/all_gather | solution.py:44
  20.9 28.3 %collective-permute-start = (bf16[2,256,1024]{2,1,0:T(8,128)(2,1)S(1)}, bf16[2,256,1024]{2,1,0:T(8,128)(2,1)S(1)}, u32[]{:S(2)}, u32[]{:S(2)}) collective-permute-start(bf16[2,256,1024]{2,1,0:T(8,128)(2,1)S(1)} %copy-done), channel_id=1, source_target_pairs={{0,1},{1,2},{2,3},{3,0},{4,5},{5,6},{6,7},{7,4},{8,9},{9,10},{10,1... | collective-permute-start | bytes 3145736 | tf_op jit(solution)/shard_map/ppermute | solution.py:25
  49.2 26.1 %collective-permute-start.1 = (bf16[2,256,1024]{2,1,0:T(8,128)(2,1)S(1)}, bf16[2,256,1024]{2,1,0:T(8,128)(2,1)S(1)}, u32[]{:S(2)}, u32[]{:S(2)}) collective-permute-start(bf16[2,256,1024]{2,1,0:T(8,128)(2,1)S(1)} %collective-permute-done), channel_id=1, source_target_pairs={{0,1},{1,2},{2,3},{3,0},{4,5},{5,6},{6,7},{7,4},{8,9},{9,10},{10,1... | collective-permute-start | bytes 3145736 | tf_op jit(solution)/shard_map/ppermute | solution.py:25
  75.3 25.4 %collective-permute-start.2 = (bf16[2,256,1024]{2,1,0:T(8,128)(2,1)S(1)}, bf16[2,256,1024]{2,1,0:T(8,128)(2,1)}, u32[]{:S(2)}, u32[]{:S(2)}) collective-permute-start(bf16[2,256,1024]{2,1,0:T(8,128)(2,1)S(1)} %collective-permute-done.1), channel_id=1, source_target_pairs={{0,1},{1,2},{2,3},{3,0},{4,5},{5,6},{6,7},{7,4},{8,9},{9,10},{10,1... | collective-permute-start | bytes 3145736 | tf_op jit(solution)/shard_map/ppermute | solution.py:25
  75.4 193.4 %all-reduce.2.cloned.1.call-start = ((), (), s32[]{:S(2)}) async-start(), calls=%async_computation.4 | async-start | bytes 1048576 | tf_op jit(solution)/shard_map/psum | solution.py:35
  231.7 3.4 copy-start.2
  234.2 94.4 %all-gather.8.cloned.1.call-start = ((), (), s32[]{:S(2)}) async-start(), calls=%async_computation.6 | async-start | bytes 10485760 | tf_op jit(solution)/shard_map/all_gather | solution.py:65
  234.8 126.9 %reduce-scatter.5.cloned.1.call-start = ((), (), s32[]{:S(2)}) async-start(), calls=%async_computation.7 | async-start | bytes 1310720 | tf_op jit(solution)/shard_map/reduce_scatter | solution.py:69
  249.9 111.9 %copy-start.1 = (bf16[4,32,1024]{2,1,0:T(8,128)(2,1)S(1)}, bf16[4,32,1024]{2,1,0:T(8,128)(2,1)}, u32[]{:S(2)}) copy-start(bf16[4,32,1024]{2,1,0:T(8,128)(2,1)} %reduce-scatter.3.cloned.1.call-done) | copy-start | bytes 786436
Sparse Core Ops, SparseCore 0:
  20.2 27.4 reduce-scatter.2
  49.3 154.7 all-gather.3
  205.7 27.9 all-gather.5
  236.0 32.7 all-reduce.1
  270.2 58.3 all-gather.7
  334.4 27.2 reduce-scatter.4
